TPU v7x, 32 devices: a whole 2x2x4 slice. The times are simulated.
32 devices in a mesh: groups: 2 (over x), hour: 16 (over z, y, core).
Axes of the slice: x: 2, y: 2, z: 4, core: 2. Of those that a mesh axis runs over, the one named last changes fastest.
Arguments:
- power: float32 [32, 16, 2048], P('groups', 'hour'), parts along dimension 0, may hold values from -3 to 3
- capacity: float32 [4096], P(('groups', 'hour')), parts along dimension 0, may hold values from 0.01 to 20
- flow_dual: float32 [32, 16, 4096], P('groups', 'hour'), parts along dimension 0, may hold values from -3 to 3
- upper_dual: float32 [32, 16, 2048], P('groups', 'hour'), parts along dimension 0, may hold values from 0 to 0.1
- lower_dual: float32 [32, 16, 2048], P('groups', 'hour'), parts along dimension 0, may hold values from 0 to 0.1
- price: float32 [32, 16], P('groups', 'hour'), parts along dimension 0, may hold values from -5 to 5
- load: bfloat16 [32, 16, 512], P('groups', 'hour'), parts along dimension 0, may hold values from -5 to 5
- shift_factors: bfloat16 [4096, 512], replicated, may hold values from -0.25 to 0.25
- line_limit: float32 [4096], replicated, may hold values from 0.5 to 3
- unit_bus: int32 [2048], replicated, may hold values from 0 to 511
- leakage: float32 [2048], replicated, may hold values from 0.015625 to 0.0625
- initial_state: float32 [4096], P('groups'), parts along dimension 0, may hold values from 0 to 10
- power_limit: float32 [2048], replicated, may hold values from 0.5 to 1.5
- capacity_cost: float32 [2048], replicated, may hold values from 0 to 0.1
Outputs:
- new_power: float32 [32, 16, 2048], P('groups', 'hour'), parts along dimension 0
- new_capacity: float32 [4096], P(('groups', 'hour')), parts along dimension 0
- new_flow_dual: float32 [32, 16, 4096], P('groups', 'hour'), parts along dimension 0
- new_upper_dual: float32 [32, 16, 2048], P('groups', 'hour'), parts along dimension 0
- new_lower_dual: float32 [32, 16, 2048], P('groups', 'hour'), parts along dimension 0
There are 2 independent parts, one for each index of `groups`. A program takes and returns all parts, laid end to end along the dimension named above; an argument that names none is the same for every part. Nothing has to cross between parts.
All inputs are finite; a program needn't handle non-finite values.
Results may differ from a plain program's by a relative error of at most 0.00093.
Values sent between devices are 32-bit elements; how exact they have to be, the bound alone decides.
A program may use at most 128 MiB of HBM per device.

v0:
```python
import functools

import jax
import jax.numpy as jnp
from jax import lax
from jax.experimental import pallas as pl
from jax.experimental.pallas import tpu as pltpu
from jax.sharding import PartitionSpec as P

ITERS = 4

primal_step = 0.05
dual_step = 0.01


def kernel(n, *refs):
    arrived, refs = refs[:14], refs[14:]
    (power_out, capacity_out, flow_out, upper_out, lower_out), refs = refs[:5], refs[5:]
    held, refs = refs[:14], refs[14:]
    (
        power_in,
        capacity_in,
        flow_in,
        upper_in,
        lower_in,
        price_in,
        load_in,
        shift,
        limit_in,
        bus_in,
        leak_in,
        start_in,
        plimit_in,
        cost_in,
    ) = held
    (
        inc,
        power,
        grid,
        flow,
        bar16,
        upper,
        lower,
        upper_stage,
        lower_stage,
        adj,
        adj_got,
        bar,
        bar_got,
        send_sems,
        recv_sems,
        load_sems,
    ) = refs
    me = lax.axis_index("hour")
    scen, hdev, units = power_in.shape
    lines, buses = shift.shape
    ud = units // n
    hours = hdev * n
    loads = [
        pltpu.make_async_copy(src, dst, load_sems.at[i])
        for i, (src, dst) in enumerate(zip(arrived, held))
    ]
    first = (3, 4)
    for i in first:
        loads[i].start()

    def peer_of(k):
        return me ^ k

    def copy_to(src, dst, channel, peer):
        return pltpu.make_async_remote_copy(
            src_ref=src.at[peer],
            dst_ref=dst.at[me],
            send_sem=send_sems.at[channel, peer],
            recv_sem=recv_sems.at[channel, me],
            device_id={"hour": peer},
            device_id_type=pl.DeviceIdType.MESH,
        )

    def wait_from(dst, channel, source):
        pltpu.make_async_remote_copy(
            src_ref=dst.at[source],
            dst_ref=dst.at[source],
            send_sem=send_sems.at[channel, source],
            recv_sem=recv_sems.at[channel, source],
            device_id={"hour": source},
            device_id_type=pl.DeviceIdType.MESH,
        ).wait_recv()

    blocks = sorted(range(1, n // 4), key=lambda z: -min(z, n // 4 - z))
    order = [z * 4 + low for low in (2, 3, 0, 1) for z in blocks] + [2, 3, 1]
    assert n % 4 == 0 and n & (n - 1) == 0 and sorted(order) == list(range(1, n))

    def each(order, function):
        for k in order:
            function(k)

    def rows_of(ref, lanes):
        return jnp.concatenate([ref[:, j, lanes] for j in range(hdev)], axis=0)

    barrier = pltpu.get_barrier_semaphore()
    each(
        order,
        lambda k: pl.semaphore_signal(
            barrier,
            inc=1,
            device_id={"hour": peer_of(k)},
            device_id_type=pl.DeviceIdType.MESH,
        ),
    )
    for i in (9, 0, 2, 7, 1, 5, 6, 8, 10, 11, 12, 13):
        loads[i].start()
    for i in first:
        loads[i].wait()
    for d in range(n):
        lanes = slice(d * ud, (d + 1) * ud)
        upper_stage[d] = rows_of(upper_in, lanes)
        lower_stage[d] = upper_stage[d] - rows_of(lower_in, lanes)
    pl.semaphore_wait(barrier, n - 1)

    each(order, lambda k: copy_to(lower_stage, lower, 1, peer_of(k)).start())
    each(order, lambda k: copy_to(upper_stage, upper, 0, peer_of(k)).start())
    upper[me] = upper_stage[me]
    lower[me] = lower_stage[me]
    for i in range(14):
        if i not in first and i != 7:
            loads[i].wait()
    for d in range(n):
        power[d] = rows_of(power_in, slice(d * ud, (d + 1) * ud))
    for j in range(hdev):
        flow[j * scen : (j + 1) * scen, :] = flow_in[:, j, :]
    piece = 128
    names = bus_in[...]
    for b in range(0, buses, piece):
        rows = lax.broadcasted_iota(jnp.int32, (piece, units), 0) + b
        inc[b : b + piece, :] = jnp.where(rows == names, 1.0, 0.0).astype(jnp.bfloat16)
    capacity_out[...] = capacity_in[...]
    retain = 1.0 - leak_in[pl.ds(me, 1), :]
    begin = start_in[pl.ds(me, 1), :]
    cost = cost_in[pl.ds(me, 1), :]
    eye = lax.broadcasted_iota(jnp.int32, (scen, scen), 0) == lax.broadcasted_iota(
        jnp.int32, (scen, scen), 1
    )
    price = jnp.concatenate(
        [
            jnp.sum(jnp.where(eye, price_in[j : j + 1, :], 0.0), axis=1, keepdims=True)
            for j in range(hdev)
        ],
        axis=0,
    )
    loads[7].wait()

    def place(t):
        return t // hdev, slice((t % hdev) * scen, (t % hdev + 1) * scen)

    def adjoint(difference):
        w = jnp.zeros((scen, ud), jnp.float32)
        for t in reversed(range(hours)):
            d, rows = place(t)
            w = retain * w + difference(d, rows)
            adj[d, rows, :] = w
        each(order, lambda k: copy_to(adj, adj_got, 2, peer_of(k)).start())
        adj_got[me] = adj[me]

    def iteration(first):
        bus_dual = jnp.dot(
            flow[...].astype(jnp.bfloat16), shift[...], preferred_element_type=jnp.float32
        ).astype(jnp.bfloat16)
        grid_grad = jnp.dot(bus_dual, inc[...], preferred_element_type=jnp.float32)
        for d in range(n):
            grid[d] = grid_grad[:, d * ud : (d + 1) * ud]

        def advance(d):
            limit = plimit_in[pl.ds(d, 1), :]
            old = power[d]
            trial = jnp.clip(
                old - primal_step * (grid[d] - adj_got[d] - price), -limit, limit
            )
            bar[d] = 2.0 * trial - old
            power[d] = trial

        advance(me)
        bar_got[me] = bar[me]

        def answer(k):
            source = peer_of(k)
            wait_from(adj_got, 2, source)
            advance(source)
            copy_to(bar, bar_got, 3, source).start()

        each(order, answer)
        for d in range(n):
            bar16[:, d * ud : (d + 1) * ud] = bar[d].astype(jnp.bfloat16)
        injection = lax.dot_general(
            bar16[...], inc[...], (((1,), (1,)), ((), ())), preferred_element_type=jnp.float32
        )
        load = jnp.concatenate([load_in[j] for j in range(hdev)], axis=0)
        injection = (injection - load.astype(jnp.float32)).astype(jnp.bfloat16)
        width = min(1024, lines)
        for c in range(0, lines, width):
            flows = lax.dot_general(
                injection,
                shift[c : c + width, :],
                (((1,), (1,)), ((), ())),
                preferred_element_type=jnp.float32,
            )
            probe = flow[:, c : c + width] + dual_step * flows
            edge = dual_step * limit_in[:, c : c + width]
            flow[:, c : c + width] = probe - jnp.clip(probe, -edge, edge)

        if first:

            def wait_upper(k):
                wait_from(upper, 0, peer_of(k))
                copy_to(upper_stage, upper, 0, peer_of(k)).wait_send()
                copy_to(lower_stage, lower, 1, peer_of(k)).wait_send()

            each(order, wait_upper)
            for d in range(n):
                lower[d] = upper[d] - lower[d]
        total = jnp.zeros((scen, ud), jnp.float32)
        for t in range(hours):
            d, rows = place(t)
            total = total + upper[d, rows, :]
        dual_total = jnp.sum(total, axis=0, keepdims=True)
        capacity = capacity_out[...]
        trial_capacity = jnp.maximum(
            capacity - primal_step * (hours * cost - dual_total / scen), 0.0
        )
        capacity_bar = 2.0 * trial_capacity - capacity
        capacity_out[...] = trial_capacity

        def wait_bar(k):
            wait_from(bar_got, 3, peer_of(k))
            copy_to(adj, adj_got, 2, peer_of(k)).wait_send()
            copy_to(bar, bar_got, 3, peer_of(k)).wait_send()

        each(order, wait_bar)
        e = jnp.broadcast_to(begin, (scen, ud))
        for t in range(hours):
            d, rows = place(t)
            e = retain * e - bar_got[d, rows, :]
            upper[d, rows, :] = jnp.maximum(
                upper[d, rows, :] + dual_step * (e - capacity_bar), 0.0
            )
            lower[d, rows, :] = jnp.maximum(lower[d, rows, :] - dual_step * e, 0.0)

    each(order, lambda k: wait_from(lower, 1, peer_of(k)))
    adjoint(lambda d, rows: lower[d, rows, :])
    iteration(True)

    def again(step, carry):
        adjoint(lambda d, rows: upper[d, rows, :] - lower[d, rows, :])
        iteration(False)
        return carry

    lax.fori_loop(1, ITERS, again, 0)

    def send_last(k):
        copy_to(upper, adj_got, 2, peer_of(k)).start()
        copy_to(lower, lower_stage, 0, peer_of(k)).start()

    each(order, send_last)
    adj_got[me] = upper[me]
    lower_stage[me] = lower[me]
    for d in range(n):
        for j in range(hdev):
            power_out[:, j, d * ud : (d + 1) * ud] = power[d, j * scen : (j + 1) * scen, :]
    for j in range(hdev):
        flow_out[:, j, :] = flow[j * scen : (j + 1) * scen, :]

    def wait_last(k):
        wait_from(adj_got, 2, peer_of(k))
        wait_from(lower_stage, 0, peer_of(k))
        copy_to(upper, adj_got, 2, peer_of(k)).wait_send()
        copy_to(lower, lower_stage, 0, peer_of(k)).wait_send()

    each(order, wait_last)
    for d in range(n):
        for j in range(hdev):
            lanes, rows = slice(d * ud, (d + 1) * ud), slice(j * scen, (j + 1) * scen)
            upper_out[:, j, lanes] = adj_got[d, rows, :]
            lower_out[:, j, lanes] = lower_stage[d, rows, :]


def store(*refs):
    sems = refs[10]
    copies = [
        pltpu.make_async_copy(refs[i], refs[5 + i], sems.at[i]) for i in (2, 0, 3, 4, 1)
    ]
    for copy in copies:
        copy.start()
    for copy in copies:
        copy.wait()


def on_device(
    power,
    capacity,
    flow_dual,
    upper_dual,
    lower_dual,
    price,
    load,
    shift_factors,
    line_limit,
    unit_bus,
    leakage,
    initial_state,
    power_limit,
    capacity_cost,
):
    n = lax.axis_size("hour")
    scen, hdev, units = power.shape
    lines, buses = shift_factors.shape
    ud, rows = units // n, scen * hdev
    block = pltpu.VMEM((n, rows, ud), jnp.float32)
    vmem = pl.BlockSpec(memory_space=pltpu.VMEM)
    hbm = pl.BlockSpec(memory_space=pltpu.HBM)
    args = (
        power,
        capacity.reshape(1, ud),
        flow_dual,
        upper_dual,
        lower_dual,
        price.T,
        load.transpose(1, 0, 2),
        shift_factors,
        line_limit.reshape(1, lines),
        unit_bus.reshape(1, units),
        leakage.reshape(n, ud),
        initial_state.reshape(n, ud),
        power_limit.reshape(n, ud),
        capacity_cost.reshape(n, ud),
    )
    results = tuple(
        jax.ShapeDtypeStruct(args[i].shape, jnp.float32) for i in range(5)
    )
    out = pl.pallas_call(
        functools.partial(kernel, n),
        out_shape=results,
        in_specs=[hbm] * 14,
        out_specs=(vmem,) * 5,
        scratch_shapes=[pltpu.VMEM(a.shape, a.dtype) for a in args]
        + [
            pltpu.VMEM((buses, units), jnp.bfloat16),
            block,
            block,
            pltpu.VMEM((rows, lines), jnp.float32),
            pltpu.VMEM((rows, units), jnp.bfloat16),
        ]
        + [block] * 8
        + [
            pltpu.SemaphoreType.DMA((4, n)),
            pltpu.SemaphoreType.DMA((4, n)),
            pltpu.SemaphoreType.DMA((14,)),
        ],
        compiler_params=pltpu.CompilerParams(
            collective_id=0, has_side_effects=True, vmem_limit_bytes=48 * 1024 * 1024
        ),
    )(*(pltpu.with_memory_space_constraint(a, pltpu.HBM) for a in args))
    out = pl.pallas_call(
        store,
        out_shape=results,
        in_specs=[vmem] * 5,
        out_specs=(hbm,) * 5,
        scratch_shapes=[pltpu.SemaphoreType.DMA((5,))],
        compiler_params=pltpu.CompilerParams(vmem_limit_bytes=16 * 1024 * 1024),
    )(*out)
    return (out[0], out[1].reshape(ud), out[2], out[3], out[4])


def solution(mesh):
    return jax.shard_map(
        on_device,
        mesh=mesh,
        in_specs=(
            P("groups", "hour", None),
            P(("groups", "hour")),
            P("groups", "hour", None),
            P("groups", "hour", None),
            P("groups", "hour", None),
            P("groups", "hour"),
            P("groups", "hour", None),
            P(),
            P(),
            P(),
            P(),
            P("groups"),
            P(),
            P(),
        ),
        out_specs=(
            P("groups", "hour", None),
            P(("groups", "hour")),
            P("groups", "hour", None),
            P("groups", "hour", None),
            P("groups", "hour", None),
        ),
        check_vma=False,
    )
```

profile of v0, /device:TPU:0, one launch (start us, length us, event | category | flops | bytes accessed | tf_op | source)
XLA Modules:
  0.0 56.2 jit_solution(2776622051834875410)
XLA Ops:
  0.6 54.7 %shard_map.173 = (f32[16,1,2048]{2,1,0:T(1,128)S(1)}, f32[1,128]{1,0:T(1,128)S(1)}, f32[16,1,4096]{2,1,0:T(1,128)S(1)}, f32[16,1,2048]{2,1,0:T(1,128)S(1)}, f32[16,1,2048]{2,1,0:T(1,128)S(1)}) custom-call(f32[16,1,2048]{2,1,0:T(1,128)} %refs_0_.1, f32[1,128]{1,0:T(1,128)} %bitcast.17, f32[16,1,4096]{2,1,0:T(1,128)} %refs_2_.1, f32[16,1,2048]{2,1,0:T(1,128)} %refs_3_.1, ...), custom_call_target="tpu_custom_call" | custom-call | tf_op jit(solution)/shard_map/pallas_call | solution.py:339
  55.3 0.9 %shard_map.174 = (f32[16,1,2048]{2,1,0:T(1,128)}, f32[1,128]{1,0:T(1,128)}, f32[16,1,4096]{2,1,0:T(1,128)}, f32[16,1,2048]{2,1,0:T(1,128)}, f32[16,1,2048]{2,1,0:T(1,128)}) custom-call(f32[16,1,2048]{2,1,0:T(1,128)S(1)} %get-tuple-element.15.refs_0_, f32[1,128]{1,0:T(1,128)S(1)} %get-tuple-element.16.refs_1_, f32[16,1,4096]{2,1,0:T(1,128)S(1)} %get-tuple-element.17.refs_2_, ...), custom_call_target="tpu_custom_call" | custom-call | tf_op jit(solution)/shard_map/pallas_call | solution.py:362
where the time goes:
time: 56.4 us; the launch traced here: 56.2 us
  Pallas kernels  55.5 us (98%)
  between operations  0.65 us (1%)
    pallas_call x1, Pallas kernels, on_device(): pl.pallas_call(functools.partial(kernel, n), out_shape=results, in_specs=...  54.7 us

commit v1 on v0

--- a/solution.py
+++ b/solution.py
@@ -294,6 +294,466 @@
         copy.wait()
 
 
+def kernel_rows(n, *refs):
+    hbm, refs = refs[:14], refs[14:]
+    (power_out, capacity_out, flow_out, upper_out, lower_out), refs = refs[:5], refs[5:]
+    (
+        capacity_in,
+        flow_home,
+        upper_home,
+        price_in,
+        load_in,
+        shift,
+        limit_in,
+        bus_in,
+        leak_in,
+        start_in,
+        plimit_in,
+        cost_in,
+        inc,
+        upper,
+        lower,
+        power,
+        flow_low,
+        flow_high,
+        grid,
+        bar,
+        bar16,
+        flow,
+        flow2,
+        flows1,
+        first_src,
+        first_dst,
+        cap_src,
+        cap_dst,
+        grad_src,
+        grad_dst,
+        total_src,
+        total_dst,
+        part_src,
+        part_dst,
+        last_src,
+        last_dst,
+        inj_src,
+        inj_dst,
+        cap_ref,
+        send_sems,
+        recv_sems,
+        load_sems,
+        own_sems,
+    ) = refs
+    me = lax.axis_index("hour")
+    power_hbm, flow_hbm, upper_hbm, lower_hbm = hbm[0], hbm[2], hbm[3], hbm[4]
+    hours = scen = n
+    lines, buses = shift.shape
+    ub, lb, bb = upper_home.shape[1], flow_home.shape[1], buses // 128
+    half = lb // 2
+    units = ub * 128
+
+    loads = {}
+
+    def load(name, src, dst, i):
+        loads[name] = pltpu.make_async_copy(src, dst, load_sems.at[i])
+        loads[name].start()
+
+    load("upper", upper_hbm, upper_home, 0)
+    load("price", hbm[5], price_in, 1)
+    load("flow", flow_hbm, flow_home, 2)
+    quarter = lines // 4
+    for q in range(4):
+        rows = pl.ds(q * quarter, quarter)
+        load(("shift", q), hbm[7].at[rows], shift.at[rows], 3 + q)
+
+    blocks = sorted(range(1, n // 4), key=lambda z: -min(z, n // 4 - z))
+    order = [z * 4 + low for low in (2, 3, 0, 1) for z in blocks] + [2, 3, 1]
+    assert n % 4 == 0 and n & (n - 1) == 0 and sorted(order) == list(range(1, n))
+
+    barrier = pltpu.get_barrier_semaphore()
+    for k in order:
+        pl.semaphore_signal(
+            barrier,
+            inc=1,
+            device_id={"hour": me ^ k},
+            device_id_type=pl.DeviceIdType.MESH,
+        )
+    for i, (name, src, dst) in enumerate(
+        (
+            ("load", 6, load_in),
+            ("bus", 9, bus_in),
+            ("capacity", 1, capacity_in),
+            ("cost", 13, cost_in),
+            ("leak", 10, leak_in),
+            ("plimit", 12, plimit_in),
+            ("start", 11, start_in),
+            ("limit", 8, limit_in),
+        )
+    ):
+        load(name, hbm[src], dst, 7 + i)
+    own = [
+        pltpu.make_async_copy(src, dst.at[me], own_sems.at[i])
+        for i, (src, dst) in enumerate(
+            (
+                (upper_hbm.at[me], upper),
+                (lower_hbm.at[me], lower),
+                (power_hbm.at[me], power),
+                (flow_hbm.at[me, pl.ds(0, half)], flow_low),
+                (flow_hbm.at[me, pl.ds(half, half)], flow_high),
+            )
+        )
+    ]
+    for copy in own:
+        copy.start()
+
+    def push(source, dst, channel):
+        for k in order:
+            peer = me ^ k
+            pltpu.make_async_remote_copy(
+                src_ref=source(peer),
+                dst_ref=dst.at[me],
+                send_sem=send_sems.at[channel],
+                recv_sem=recv_sems.at[channel],
+                device_id={"hour": peer},
+                device_id_type=pl.DeviceIdType.MESH,
+            ).start()
+
+    def everything(dst, channel):
+        rest = dst.at[pl.ds(0, n - 1)]
+        return pltpu.make_async_remote_copy(
+            src_ref=rest,
+            dst_ref=rest,
+            send_sem=send_sems.at[channel],
+            recv_sem=recv_sems.at[channel],
+            device_id={"hour": me ^ 1},
+            device_id_type=pl.DeviceIdType.MESH,
+        )
+
+    def arrive(dst, channel):
+        everything(dst, channel).wait_recv()
+
+    def lanes(j):
+        return slice(j * 128, (j + 1) * 128)
+
+    eye = lax.broadcasted_iota(jnp.int32, (scen, scen), 0) == lax.broadcasted_iota(
+        jnp.int32, (scen, scen), 1
+    )
+    loads["upper"].wait()
+    loads["price"].wait()
+    part = upper_home[0]
+    for s in range(1, scen):
+        part = part + upper_home[s]
+    price = jnp.sum(jnp.where(eye, price_in[...], 0.0), axis=1, keepdims=True)
+    first_src[:, 0, :] = part
+    first_src[:, 1, :] = jnp.broadcast_to(price, (scen, 128))
+    pl.semaphore_wait(barrier, n - 1)
+
+    push(lambda peer: first_src.at[peer], first_dst, 0)
+    push(lambda peer: upper_hbm.at[peer], upper, 1)
+    push(lambda peer: lower_hbm.at[peer], lower, 2)
+    push(lambda peer: power_hbm.at[peer], power, 3)
+    first_dst[me] = first_src[me]
+
+    def bus_dual(rows):
+        return jnp.dot(
+            rows.astype(jnp.bfloat16), shift[...], preferred_element_type=jnp.float32
+        ).astype(jnp.bfloat16)
+
+    loads["flow"].wait()
+    for j in range(lb):
+        flow2[:, lanes(j)] = flow_home[:, j, :]
+    for q in range(4):
+        loads[("shift", q)].wait()
+    dual = bus_dual(flow2[...]).astype(jnp.float32)
+    loads["load"].wait()
+    demand = load_in[0].astype(jnp.float32)
+    for j in range(bb):
+        grad_src[:, j, :] = dual[:, lanes(j)]
+        grad_src[:, bb + j, :] = demand[:, lanes(j)]
+    push(lambda peer: grad_src.at[peer], grad_dst, 4)
+    grad_dst[me] = grad_src[me]
+
+    loads["capacity"].wait()
+    loads["cost"].wait()
+    arrive(first_dst, 0)
+    my_cost = cost_in[pl.ds(me, 1), :]
+
+    def next_capacity(old, cost, total):
+        return jnp.maximum(old - primal_step * (hours * cost - total / scen), 0.0)
+
+    old = capacity_in[...]
+    trial = next_capacity(old, my_cost, jnp.sum(first_dst[:, 0, :], axis=0, keepdims=True))
+    cap_src[0:1, :] = trial
+    cap_src[1:2, :] = 2.0 * trial - old
+    push(lambda peer: cap_src, cap_dst, 5)
+    cap_dst[me] = cap_src[...]
+    push(lambda peer: flow_hbm.at[peer, pl.ds(0, half)], flow_low, 6)
+    push(lambda peer: flow_hbm.at[peer, pl.ds(half, half)], flow_high, 7)
+
+    for name in ("bus", "leak", "plimit", "start", "limit"):
+        loads[name].wait()
+    piece = 128
+    names = bus_in[...]
+    for b in range(0, buses, piece):
+        rows = lax.broadcasted_iota(jnp.int32, (piece, units), 0) + b
+        inc[b : b + piece, :] = jnp.where(rows == names, 1.0, 0.0).astype(jnp.bfloat16)
+    retain = 1.0 - leak_in[...]
+    plimit = plimit_in[...]
+    width = min(1024, lines)
+
+    def gradient(dual):
+        value = jnp.dot(dual, inc[...], preferred_element_type=jnp.float32)
+        for j in range(ub):
+            grid[:, j, :] = value[:, lanes(j)]
+
+    def primal():
+        w = jnp.zeros((ub, 128), jnp.float32)
+        for t in reversed(range(hours)):
+            w = retain * w + (upper[t] - lower[t])
+            old = power[t]
+            trial = jnp.clip(
+                old - primal_step * (grid[t] - w - first_dst[t, 1:2, :]), -plimit, plimit
+            )
+            bar[t] = 2.0 * trial - old
+            power[t] = trial
+
+    def states(function):
+        e = start_in[...]
+        for t in range(hours):
+            e = retain * e - bar[t]
+            function(t, e)
+
+    def inject(i):
+        for j in range(ub):
+            bar16[:, lanes(j)] = bar[:, j, :].astype(jnp.bfloat16)
+        value = lax.dot_general(
+            bar16[...], inc[...], (((1,), (1,)), ((), ())), preferred_element_type=jnp.float32
+        )
+        demand = jnp.concatenate([grad_dst[:, bb + j, :] for j in range(bb)], axis=1)
+        value = (value - demand).astype(jnp.bfloat16)
+        wide = value.astype(jnp.float32)
+        for j in range(bb):
+            inj_src[i, :, j, :] = wide[:, lanes(j)]
+        push(lambda peer: inj_src.at[i, peer], inj_dst.at[i], 8 + i)
+        inj_dst[i, me] = inj_src[i, me]
+        return value
+
+    def injected(i):
+        arrive(inj_dst.at[i], 8 + i)
+        return jnp.concatenate([inj_dst[i, :, j, :] for j in range(bb)], axis=1).astype(
+            jnp.bfloat16
+        )
+
+    def line_flows(value, c):
+        return lax.dot_general(
+            value,
+            shift[c : c + width, :],
+            (((1,), (1,)), ((), ())),
+            preferred_element_type=jnp.float32,
+        )
+
+    def advance(ref, c, flows):
+        probe = ref[:, c : c + width] + dual_step * flows
+        edge = dual_step * limit_in[:, c : c + width]
+        ref[:, c : c + width] = probe - jnp.clip(probe, -edge, edge)
+
+    def update_duals(capacity_bar):
+        totals = [jnp.zeros((ub, 128), jnp.float32)]
+
+        def update(t, e):
+            raised = jnp.maximum(upper[t] + dual_step * (e - capacity_bar), 0.0)
+            upper[t] = raised
+            totals[0] = totals[0] + raised
+            lower[t] = jnp.maximum(lower[t] - dual_step * e, 0.0)
+
+        states(update)
+        return totals[0]
+
+    def broadcast(i, total):
+        total_src[i] = total
+        push(lambda peer: total_src.at[i], total_dst.at[i], 12 + i)
+        total_dst[i, me] = total
+
+    def capacity_step(i):
+        arrive(total_dst.at[i], 12 + i)
+        total = total_dst[i, 0]
+        for d in range(1, n):
+            total = total + total_dst[i, d]
+        old = cap_ref[...]
+        trial = next_capacity(old, cost_in[...], total)
+        cap_ref[...] = trial
+        return 2.0 * trial - old
+
+    for copy in own:
+        copy.wait()
+    arrive(grad_dst, 4)
+    gradient(
+        jnp.concatenate([grad_dst[:, j, :] for j in range(bb)], axis=1).astype(jnp.bfloat16)
+    )
+    arrive(upper, 1)
+    arrive(lower, 2)
+    arrive(power, 3)
+    primal()
+    arrive(cap_dst, 5)
+    cap_ref[...] = cap_dst[:, 0, :]
+    broadcast(0, update_duals(cap_dst[:, 1, :]))
+    value = inject(0)
+    for c in range(0, lines, width):
+        flows1[:, c : c + width] = line_flows(value, c)
+    for part, ref, channel in ((0, flow_low, 6), (1, flow_high, 7)):
+        arrive(ref, channel)
+        for j in range(half):
+            flow[:, lanes(part * half + j)] = ref[:, j, :]
+    for c in range(0, lines, width):
+        advance(flow, c, flows1[:, c : c + width])
+
+    for step in (1, 2):
+        gradient(bus_dual(flow[...]))
+        primal()
+        total = update_duals(capacity_step(step - 1))
+        if step == 1:
+            broadcast(1, total)
+        else:
+            part_src[:, 0, :] = total
+            push(lambda peer: part_src.at[peer], part_dst, 14)
+            part_dst[me] = part_src[me]
+        value = inject(step)
+        both = jnp.concatenate([value, injected(step - 1)], axis=0)
+        for c in range(0, lines, width):
+            flows = line_flows(both, c)
+            advance(flow, c, flows[:n])
+            advance(flow2, c, flows[n:])
+
+    gradient(bus_dual(flow[...]))
+    primal()
+    push(lambda peer: power.at[peer], power_out, 15)
+    power_out[me] = power[me]
+    inject(3)
+
+    def last(t, e):
+        upper[t] = upper[t] + dual_step * e
+        lower[t] = jnp.maximum(lower[t] - dual_step * e, 0.0)
+
+    states(last)
+    push(lambda peer: lower.at[peer], lower_out, 16)
+    push(lambda peer: upper.at[peer], upper_out, 17)
+    lower_out[me] = lower[me]
+    upper_out[me] = upper[me]
+    arrive(part_dst, 14)
+    old = cap_ref[pl.ds(me, 1), :]
+    trial = next_capacity(old, my_cost, jnp.sum(part_dst[:, 0, :], axis=0, keepdims=True))
+    capacity_out[...] = trial
+    last_src[...] = 2.0 * trial - old
+    push(lambda peer: last_src, last_dst, 18)
+    last_dst[me] = last_src[...]
+
+    for i in (2, 3):
+        value = injected(i)
+        for c in range(0, lines, width):
+            advance(flow2, c, line_flows(value, c))
+    for j in range(lb):
+        flow_out[:, j, :] = flow2[:, lanes(j)]
+    arrive(power_out, 15)
+    arrive(lower_out, 16)
+    arrive(last_dst, 18)
+    raised = dual_step * last_dst[:, 0, :]
+    arrive(upper_out, 17)
+    for s in range(scen):
+        upper_out[s] = jnp.maximum(upper_out[s] - raised, 0.0)
+    sent = (
+        [first_dst, upper, lower, power, grad_dst, cap_dst, flow_low, flow_high]
+        + [inj_dst.at[i] for i in range(4)]
+        + [total_dst.at[i] for i in range(2)]
+        + [part_dst, power_out, lower_out, upper_out, last_dst]
+    )
+    for channel, dst in enumerate(sent):
+        everything(dst, channel).wait_send()
+
+
+def by_rows(n, args):
+    power, capacity, flow, upper, lower, price, load, shift, limit, bus = args[:10]
+    leak, start, plimit, cost = args[10:]
+    scen, _, units = power.shape
+    lines, buses = shift.shape
+    ub, lb, bb = units // 128, lines // 128, buses // 128
+    vmem = pl.BlockSpec(memory_space=pltpu.VMEM)
+    hbm = pl.BlockSpec(memory_space=pltpu.HBM)
+    state, wide = (scen, ub, 128), (scen, lb, 128)
+    args = (
+        power.reshape(state),
+        capacity,
+        flow.reshape(wide),
+        upper.reshape(state),
+        lower.reshape(state),
+        price,
+        load,
+        shift,
+        limit,
+        bus,
+        leak,
+        start,
+        plimit,
+        cost,
+    )
+    f32 = jnp.float32
+    results = tuple(jax.ShapeDtypeStruct(args[i].shape, f32) for i in range(5))
+
+    def buffer(*shape, dtype=f32):
+        return pltpu.VMEM(shape, dtype)
+
+    out = pl.pallas_call(
+        functools.partial(kernel_rows, n),
+        out_shape=results,
+        in_specs=[hbm] * 14,
+        out_specs=(vmem,) * 5,
+        scratch_shapes=[pltpu.VMEM(args[i].shape, args[i].dtype) for i in (1, 2, 3)]
+        + [pltpu.VMEM(a.shape, a.dtype) for a in args[5:]]
+        + [buffer(buses, units, dtype=jnp.bfloat16)]
+        + [buffer(*state)] * 3
+        + [buffer(n, lb // 2, 128)] * 2
+        + [buffer(*state)] * 2
+        + [buffer(n, units, dtype=jnp.bfloat16)]
+        + [buffer(n, lines)] * 3
+        + [
+            buffer(n, 2, 128),
+            buffer(n, 2, 128),
+            buffer(2, 128),
+            buffer(n, 2, 128),
+            buffer(n, 2 * bb, 128),
+            buffer(n, 2 * bb, 128),
+            buffer(2, ub, 128),
+            buffer(2, n, ub, 128),
+            buffer(n, 1, 128),
+            buffer(n, 1, 128),
+            buffer(1, 128),
+            buffer(n, 1, 128),
+            buffer(4, n, bb, 128),
+            buffer(4, n, bb, 128),
+            buffer(ub, 128),
+            pltpu.SemaphoreType.DMA((19,)),
+            pltpu.SemaphoreType.DMA((19,)),
+            pltpu.SemaphoreType.DMA((15,)),
+            pltpu.SemaphoreType.DMA((5,)),
+        ],
+        compiler_params=pltpu.CompilerParams(
+            collective_id=0, has_side_effects=True, vmem_limit_bytes=48 * 1024 * 1024
+        ),
+    )(*(pltpu.with_memory_space_constraint(a, pltpu.HBM) for a in args))
+    out = pl.pallas_call(
+        store,
+        out_shape=results,
+        in_specs=[vmem] * 5,
+        out_specs=(hbm,) * 5,
+        scratch_shapes=[pltpu.SemaphoreType.DMA((5,))],
+        compiler_params=pltpu.CompilerParams(vmem_limit_bytes=16 * 1024 * 1024),
+    )(*out)
+    return (
+        out[0].reshape(power.shape),
+        out[1].reshape(units // n),
+        out[2].reshape(flow.shape),
+        out[3].reshape(upper.shape),
+        out[4].reshape(lower.shape),
+    )
+
+
 def on_device(
     power,
     capacity,
@@ -333,6 +793,8 @@
         power_limit.reshape(n, ud),
         capacity_cost.reshape(n, ud),
     )
+    if scen == n and hdev == 1 and ud == 128 and lines % 1024 == 0 and buses % 128 == 0:
+        return by_rows(n, args)
     results = tuple(
         jax.ShapeDtypeStruct(args[i].shape, jnp.float32) for i in range(5)
     )

time: 56.4 us -> 49.8 us (0.88)
  Pallas kernels: 55.5 us -> 48.9 us
    pallas_call x2, Pallas kernels: 55.5 us -> 48.9 us  [the longest x1 48.1 us: by_rows(): pl.pallas_call(functools.partial(kernel_rows, n), out_shape=results, in_s...]
where the time goes in v1:
time: 49.8 us; the launch traced here: 49.6 us
  Pallas kernels  48.9 us (98%)
  between operations  0.65 us (1%)
    pallas_call x1, Pallas kernels, by_rows(): pl.pallas_call(functools.partial(kernel_rows, n), out_shape=results, in_s...  48.1 us

profile of v1, /device:TPU:0, one launch (start us, length us, event | category | flops | bytes accessed | tf_op | source)
XLA Modules:
  0.0 49.6 jit_solution(5121836664482158476)
XLA Ops:
  0.6 48.1 %shard_map.173 = (f32[16,16,128]{2,1,0:T(8,128)S(1)}, f32[1,128]{1,0:T(1,128)S(1)}, f32[16,32,128]{2,1,0:T(8,128)S(1)}, f32[16,16,128]{2,1,0:T(8,128)S(1)}, f32[16,16,128]{2,1,0:T(8,128)S(1)}) custom-call(f32[16,16,128]{2,1,0:T(8,128)} %bitcast.19, f32[1,128]{1,0:T(1,128)} %bitcast.29, f32[16,32,128]{2,1,0:T(8,128)} %bitcast.18, f32[16,16,128]{2,1,0:T(8,128)} %bitcast.20, ...), custom_call_target="tpu_custom_call" | custom-call | tf_op jit(solution)/shard_map/pallas_call | solution.py:702
  48.7 0.9 %shard_map.174 = (f32[16,16,128]{2,1,0:T(8,128)}, f32[1,128]{1,0:T(1,128)}, f32[16,32,128]{2,1,0:T(8,128)}, f32[16,16,128]{2,1,0:T(8,128)}, f32[16,16,128]{2,1,0:T(8,128)}) custom-call(f32[16,16,128]{2,1,0:T(8,128)S(1)} %get-tuple-element.15.refs_0_, f32[1,128]{1,0:T(1,128)S(1)} %get-tuple-element.16.refs_1_, f32[16,32,128]{2,1,0:T(8,128)S(1)} %get-tuple-element.17.refs_2_, ...), custom_call_target="tpu_custom_call" | custom-call | tf_op jit(solution)/shard_map/pallas_call | solution.py:740

commit v2 on v1

--- a/solution.py
+++ b/solution.py
@@ -311,11 +311,12 @@
         plimit_in,
         cost_in,
         inc,
+        inc_t,
+        shift_t,
         upper,
         lower,
         power,
-        flow_low,
-        flow_high,
+        flow_in,
         grid,
         bar,
         bar16,
@@ -329,6 +330,8 @@
         grad_src,
         grad_dst,
         total_src,
+        pair_dst,
+        chip_src,
         total_dst,
         part_src,
         part_dst,
@@ -336,9 +339,15 @@
         last_dst,
         inj_src,
         inj_dst,
+        state,
+        power_home,
+        adjoint,
+        adjoint_home,
         cap_ref,
         send_sems,
         recv_sems,
+        pair_send,
+        pair_recv,
         load_sems,
         own_sems,
     ) = refs
@@ -347,22 +356,8 @@
     hours = scen = n
     lines, buses = shift.shape
     ub, lb, bb = upper_home.shape[1], flow_home.shape[1], buses // 128
-    half = lb // 2
+    quarter_lb = lb // 4
     units = ub * 128
-
-    loads = {}
-
-    def load(name, src, dst, i):
-        loads[name] = pltpu.make_async_copy(src, dst, load_sems.at[i])
-        loads[name].start()
-
-    load("upper", upper_hbm, upper_home, 0)
-    load("price", hbm[5], price_in, 1)
-    load("flow", flow_hbm, flow_home, 2)
-    quarter = lines // 4
-    for q in range(4):
-        rows = pl.ds(q * quarter, quarter)
-        load(("shift", q), hbm[7].at[rows], shift.at[rows], 3 + q)
 
     blocks = sorted(range(1, n // 4), key=lambda z: -min(z, n // 4 - z))
     order = [z * 4 + low for low in (2, 3, 0, 1) for z in blocks] + [2, 3, 1]
@@ -376,6 +371,20 @@
             device_id={"hour": me ^ k},
             device_id_type=pl.DeviceIdType.MESH,
         )
+    loads = {}
+
+    def load(name, src, dst, i):
+        loads[name] = pltpu.make_async_copy(src, dst, load_sems.at[i])
+        loads[name].start()
+
+    load("upper", upper_hbm, upper_home, 0)
+    load("price", hbm[5], price_in, 1)
+    load("flow", flow_hbm, flow_home, 2)
+    quarter = lines // 4
+    for q in range(4):
+        rows = pl.ds(q * quarter, quarter)
+        load(("shift", q), hbm[7].at[rows], shift.at[rows], 3 + q)
+
     for i, (name, src, dst) in enumerate(
         (
             ("load", 6, load_in),
@@ -396,8 +405,10 @@
                 (upper_hbm.at[me], upper),
                 (lower_hbm.at[me], lower),
                 (power_hbm.at[me], power),
-                (flow_hbm.at[me, pl.ds(0, half)], flow_low),
-                (flow_hbm.at[me, pl.ds(half, half)], flow_high),
+            )
+            + tuple(
+                (flow_hbm.at[me, pl.ds(q * quarter_lb, quarter_lb)], flow_in.at[q])
+                for q in range(4)
             )
         )
     ]
@@ -448,8 +459,6 @@
 
     push(lambda peer: first_src.at[peer], first_dst, 0)
     push(lambda peer: upper_hbm.at[peer], upper, 1)
-    push(lambda peer: lower_hbm.at[peer], lower, 2)
-    push(lambda peer: power_hbm.at[peer], power, 3)
     first_dst[me] = first_src[me]
 
     def bus_dual(rows):
@@ -485,8 +494,8 @@
     cap_src[1:2, :] = 2.0 * trial - old
     push(lambda peer: cap_src, cap_dst, 5)
     cap_dst[me] = cap_src[...]
-    push(lambda peer: flow_hbm.at[peer, pl.ds(0, half)], flow_low, 6)
-    push(lambda peer: flow_hbm.at[peer, pl.ds(half, half)], flow_high, 7)
+    push(lambda peer: lower_hbm.at[peer], lower, 2)
+    push(lambda peer: power_hbm.at[peer], power, 3)
 
     for name in ("bus", "leak", "plimit", "start", "limit"):
         loads[name].wait()
@@ -497,6 +506,10 @@
         inc[b : b + piece, :] = jnp.where(rows == names, 1.0, 0.0).astype(jnp.bfloat16)
     retain = 1.0 - leak_in[...]
     plimit = plimit_in[...]
+    for b in range(0, buses, piece):
+        inc_t[:, b : b + piece] = inc[b : b + piece, :].T
+    for c in range(0, lines, 512):
+        shift_t[:, c : c + 512] = shift[c : c + 512, :].T
     width = min(1024, lines)
 
     def gradient(dual):
@@ -504,37 +517,47 @@
         for j in range(ub):
             grid[:, j, :] = value[:, lanes(j)]
 
-    def primal():
+    def adjoints():
         w = jnp.zeros((ub, 128), jnp.float32)
         for t in reversed(range(hours)):
             w = retain * w + (upper[t] - lower[t])
-            old = power[t]
+            adjoint[t] = w
+
+    def primal(old_from, dual_from, prices, new_to):
+        for t in range(hours):
+            old = old_from[t]
             trial = jnp.clip(
-                old - primal_step * (grid[t] - w - first_dst[t, 1:2, :]), -plimit, plimit
+                old - primal_step * (grid[t] - dual_from[t] - prices[t, 1:2, :]),
+                -plimit,
+                plimit,
             )
             bar[t] = 2.0 * trial - old
-            power[t] = trial
-
-    def states(function):
+            if new_to is not None:
+                new_to[t] = trial
+
+    def states():
         e = start_in[...]
         for t in range(hours):
             e = retain * e - bar[t]
-            function(t, e)
-
-    def inject(i):
+            state[t] = e
+
+    def injection(demand_from):
         for j in range(ub):
             bar16[:, lanes(j)] = bar[:, j, :].astype(jnp.bfloat16)
-        value = lax.dot_general(
-            bar16[...], inc[...], (((1,), (1,)), ((), ())), preferred_element_type=jnp.float32
-        )
-        demand = jnp.concatenate([grad_dst[:, bb + j, :] for j in range(bb)], axis=1)
-        value = (value - demand).astype(jnp.bfloat16)
+        value = jnp.dot(bar16[...], inc_t[...], preferred_element_type=jnp.float32)
+        demand = jnp.concatenate([demand_from[:, bb + j, :] for j in range(bb)], axis=1)
+        return (value - demand).astype(jnp.bfloat16)
+
+    def inject(i):
+        value = injection(grad_dst)
         wide = value.astype(jnp.float32)
         for j in range(bb):
             inj_src[i, :, j, :] = wide[:, lanes(j)]
+        return value
+
+    def send_injection(i):
         push(lambda peer: inj_src.at[i, peer], inj_dst.at[i], 8 + i)
         inj_dst[i, me] = inj_src[i, me]
-        return value
 
     def injected(i):
         arrive(inj_dst.at[i], 8 + i)
@@ -543,40 +566,59 @@
         )
 
     def line_flows(value, c):
-        return lax.dot_general(
-            value,
-            shift[c : c + width, :],
-            (((1,), (1,)), ((), ())),
-            preferred_element_type=jnp.float32,
-        )
+        return jnp.dot(value, shift_t[:, c : c + width], preferred_element_type=jnp.float32)
 
     def advance(ref, c, flows):
         probe = ref[:, c : c + width] + dual_step * flows
         edge = dual_step * limit_in[:, c : c + width]
         ref[:, c : c + width] = probe - jnp.clip(probe, -edge, edge)
 
+    def lines_step(ref, value):
+        for c in range(0, lines, width):
+            advance(ref, c, line_flows(value, c))
+
     def update_duals(capacity_bar):
-        totals = [jnp.zeros((ub, 128), jnp.float32)]
-
-        def update(t, e):
+        total = jnp.zeros((ub, 128), jnp.float32)
+        for t in range(hours):
+            e = state[t]
             raised = jnp.maximum(upper[t] + dual_step * (e - capacity_bar), 0.0)
             upper[t] = raised
-            totals[0] = totals[0] + raised
+            total = total + raised
             lower[t] = jnp.maximum(lower[t] - dual_step * e, 0.0)
-
-        states(update)
-        return totals[0]
-
-    def broadcast(i, total):
-        total_src[i] = total
-        push(lambda peer: total_src.at[i], total_dst.at[i], 12 + i)
-        total_dst[i, me] = total
+        return total
+
+    hb = ub // 2
+    side = me % 2
+
+    def pair_copy(i):
+        return pltpu.make_async_remote_copy(
+            src_ref=total_src.at[i, 1 - side],
+            dst_ref=pair_dst.at[i],
+            send_sem=pair_send.at[i],
+            recv_sem=pair_recv.at[i],
+            device_id={"hour": me ^ 1},
+            device_id_type=pl.DeviceIdType.MESH,
+        )
+
+    def pair_up(i, total):
+        total_src[i, 0] = total[:hb]
+        total_src[i, 1] = total[hb:]
+        pair_copy(i).start()
+
+    def broadcast(i):
+        pair_copy(i).wait_recv()
+        chip = total_src[i, side] + pair_dst[i]
+        chip_src[i] = chip
+        push(lambda peer: chip_src.at[i], total_dst.at[i], 11 + i)
+        total_dst[i, me] = chip
 
     def capacity_step(i):
-        arrive(total_dst.at[i], 12 + i)
-        total = total_dst[i, 0]
-        for d in range(1, n):
-            total = total + total_dst[i, d]
+        arrive(total_dst.at[i], 11 + i)
+        low, high = total_dst[i, 0], total_dst[i, 1]
+        for d in range(2, n, 2):
+            low = low + total_dst[i, d]
+            high = high + total_dst[i, d + 1]
+        total = jnp.concatenate([low, high], axis=0)
         old = cap_ref[...]
         trial = next_capacity(old, cost_in[...], total)
         cap_ref[...] = trial
@@ -584,88 +626,115 @@
 
     for copy in own:
         copy.wait()
+
+    def push_flow(q):
+        push(
+            lambda peer: flow_hbm.at[peer, pl.ds(q * quarter_lb, quarter_lb)],
+            flow_in.at[q],
+            (6, 7, 19, 20)[q],
+        )
+
+    arrive(upper, 1)
     arrive(grad_dst, 4)
+    push_flow(0)
+    push_flow(1)
+    arrive(lower, 2)
+    push_flow(2)
+    arrive(power, 3)
+    push_flow(3)
     gradient(
         jnp.concatenate([grad_dst[:, j, :] for j in range(bb)], axis=1).astype(jnp.bfloat16)
     )
-    arrive(upper, 1)
-    arrive(lower, 2)
-    arrive(power, 3)
-    primal()
+    adjoints()
+    primal(power, adjoint, first_dst, power)
+    states()
     arrive(cap_dst, 5)
     cap_ref[...] = cap_dst[:, 0, :]
-    broadcast(0, update_duals(cap_dst[:, 1, :]))
+    pair_up(0, update_duals(cap_dst[:, 1, :]))
     value = inject(0)
+    broadcast(0)
+    send_injection(0)
+    adjoints()
     for c in range(0, lines, width):
         flows1[:, c : c + width] = line_flows(value, c)
-    for part, ref, channel in ((0, flow_low, 6), (1, flow_high, 7)):
-        arrive(ref, channel)
-        for j in range(half):
-            flow[:, lanes(part * half + j)] = ref[:, j, :]
-    for c in range(0, lines, width):
-        advance(flow, c, flows1[:, c : c + width])
-
-    for step in (1, 2):
-        gradient(bus_dual(flow[...]))
-        primal()
-        total = update_duals(capacity_step(step - 1))
-        if step == 1:
-            broadcast(1, total)
-        else:
-            part_src[:, 0, :] = total
-            push(lambda peer: part_src.at[peer], part_dst, 14)
-            part_dst[me] = part_src[me]
-        value = inject(step)
-        both = jnp.concatenate([value, injected(step - 1)], axis=0)
-        for c in range(0, lines, width):
-            flows = line_flows(both, c)
-            advance(flow, c, flows[:n])
-            advance(flow2, c, flows[n:])
+    for q in range(4):
+        arrive(flow_in.at[q], (6, 7, 19, 20)[q])
+        for j in range(quarter_lb):
+            flow[:, lanes(q * quarter_lb + j)] = flow_in[q, :, j, :]
+        for c in range(q * quarter_lb * 128, (q + 1) * quarter_lb * 128, width):
+            advance(flow, c, flows1[:, c : c + width])
 
     gradient(bus_dual(flow[...]))
-    primal()
-    push(lambda peer: power.at[peer], power_out, 15)
-    power_out[me] = power[me]
-    inject(3)
-
-    def last(t, e):
+    primal(power, adjoint, first_dst, power)
+    states()
+    pair_up(1, update_duals(capacity_step(0)))
+    value = inject(1)
+    broadcast(1)
+    send_injection(1)
+    adjoints()
+    lines_step(flow, value)
+
+    gradient(bus_dual(flow[...]))
+    primal(power, adjoint, first_dst, power)
+    push(lambda peer: power.at[peer], power_home, 14)
+    power_home[me] = power[me]
+    states()
+    part_src[:, 0, :] = update_duals(capacity_step(1))
+    push(lambda peer: part_src.at[peer], part_dst, 13)
+    part_dst[me] = part_src[me]
+    adjoints()
+    value = inject(2)
+    send_injection(2)
+    push(lambda peer: adjoint.at[peer], adjoint_home, 15)
+    adjoint_home[me] = adjoint[me]
+    lines_step(flow, value)
+
+    gradient(bus_dual(flow[...]))
+    primal(power, adjoint, first_dst, None)
+    e = start_in[...]
+    for t in range(hours):
+        e = retain * e - bar[t]
+        lower[t] = jnp.maximum(lower[t] - dual_step * e, 0.0)
         upper[t] = upper[t] + dual_step * e
-        lower[t] = jnp.maximum(lower[t] - dual_step * e, 0.0)
-
-    states(last)
     push(lambda peer: lower.at[peer], lower_out, 16)
-    push(lambda peer: upper.at[peer], upper_out, 17)
     lower_out[me] = lower[me]
     upper_out[me] = upper[me]
-    arrive(part_dst, 14)
+    arrive(part_dst, 13)
     old = cap_ref[pl.ds(me, 1), :]
     trial = next_capacity(old, my_cost, jnp.sum(part_dst[:, 0, :], axis=0, keepdims=True))
     capacity_out[...] = trial
     last_src[...] = 2.0 * trial - old
     push(lambda peer: last_src, last_dst, 18)
+    push(lambda peer: upper.at[peer], upper_out, 17)
     last_dst[me] = last_src[...]
 
-    for i in (2, 3):
-        value = injected(i)
-        for c in range(0, lines, width):
-            advance(flow2, c, line_flows(value, c))
+    lines_step(flow2, injected(0))
+    lines_step(flow2, injected(1))
+    lines_step(flow2, injected(2))
+    gradient(bus_dual(flow2[...]))
+    arrive(power_home, 14)
+    arrive(adjoint_home, 15)
+    primal(power_home, adjoint_home, first_src, power_out)
+    lines_step(flow2, injection(grad_src))
     for j in range(lb):
         flow_out[:, j, :] = flow2[:, lanes(j)]
-    arrive(power_out, 15)
     arrive(lower_out, 16)
+    arrive(upper_out, 17)
     arrive(last_dst, 18)
     raised = dual_step * last_dst[:, 0, :]
-    arrive(upper_out, 17)
     for s in range(scen):
         upper_out[s] = jnp.maximum(upper_out[s] - raised, 0.0)
     sent = (
-        [first_dst, upper, lower, power, grad_dst, cap_dst, flow_low, flow_high]
-        + [inj_dst.at[i] for i in range(4)]
+        [first_dst, upper, lower, power, grad_dst, cap_dst, flow_in.at[0], flow_in.at[1]]
+        + [inj_dst.at[i] for i in range(3)]
         + [total_dst.at[i] for i in range(2)]
-        + [part_dst, power_out, lower_out, upper_out, last_dst]
+        + [part_dst, power_home, adjoint_home, lower_out, upper_out, last_dst]
+        + [flow_in.at[2], flow_in.at[3]]
     )
     for channel, dst in enumerate(sent):
         everything(dst, channel).wait_send()
+    for i in range(2):
+        pair_copy(i).wait_send()
 
 
 def by_rows(n, args):
@@ -707,8 +776,10 @@
         scratch_shapes=[pltpu.VMEM(args[i].shape, args[i].dtype) for i in (1, 2, 3)]
         + [pltpu.VMEM(a.shape, a.dtype) for a in args[5:]]
         + [buffer(buses, units, dtype=jnp.bfloat16)]
+        + [buffer(units, buses, dtype=jnp.bfloat16)]
+        + [buffer(buses, lines, dtype=jnp.bfloat16)]
         + [buffer(*state)] * 3
-        + [buffer(n, lb // 2, 128)] * 2
+        + [buffer(4, n, lb // 4, 128)]
         + [buffer(*state)] * 2
         + [buffer(n, units, dtype=jnp.bfloat16)]
         + [buffer(n, lines)] * 3
@@ -719,19 +790,27 @@
             buffer(n, 2, 128),
             buffer(n, 2 * bb, 128),
             buffer(n, 2 * bb, 128),
-            buffer(2, ub, 128),
-            buffer(2, n, ub, 128),
+            buffer(2, 2, ub // 2, 128),
+            buffer(2, ub // 2, 128),
+            buffer(2, ub // 2, 128),
+            buffer(2, n, ub // 2, 128),
             buffer(n, 1, 128),
             buffer(n, 1, 128),
             buffer(1, 128),
             buffer(n, 1, 128),
-            buffer(4, n, bb, 128),
-            buffer(4, n, bb, 128),
+            buffer(3, n, bb, 128),
+            buffer(3, n, bb, 128),
+            buffer(*state),
+            buffer(*state),
+            buffer(*state),
+            buffer(*state),
             buffer(ub, 128),
-            pltpu.SemaphoreType.DMA((19,)),
-            pltpu.SemaphoreType.DMA((19,)),
+            pltpu.SemaphoreType.DMA((21,)),
+            pltpu.SemaphoreType.DMA((21,)),
+            pltpu.SemaphoreType.DMA((2,)),
+            pltpu.SemaphoreType.DMA((2,)),
             pltpu.SemaphoreType.DMA((15,)),
-            pltpu.SemaphoreType.DMA((5,)),
+            pltpu.SemaphoreType.DMA((7,)),
         ],
         compiler_params=pltpu.CompilerParams(
             collective_id=0, has_side_effects=True, vmem_limit_bytes=48 * 1024 * 1024

time: 49.8 us -> 46.2 us (0.928)
  Pallas kernels: 48.9 us -> 45.4 us
    pallas_call x1, Pallas kernels: 48.1 us -> 44.6 us  [by_rows(): pl.pallas_call(functools.partial(kernel_rows, n), out_shape=results, in_s...]
where the time goes in v2:
time: 46.2 us; the launch traced here: 46.1 us
  Pallas kernels  45.4 us (98%)
  between operations  0.65 us (1%)
    pallas_call x1, Pallas kernels, by_rows(): pl.pallas_call(functools.partial(kernel_rows, n), out_shape=results, in_s...  44.6 us

profile of v2, /device:TPU:0, one launch (start us, length us, event | category | flops | bytes accessed | tf_op | source)
XLA Modules:
  0.0 46.1 jit_solution(11786870638904886296)
XLA Ops:
  0.6 44.6 %shard_map.173 = (f32[16,16,128]{2,1,0:T(8,128)S(1)}, f32[1,128]{1,0:T(1,128)S(1)}, f32[16,32,128]{2,1,0:T(8,128)S(1)}, f32[16,16,128]{2,1,0:T(8,128)S(1)}, f32[16,16,128]{2,1,0:T(8,128)S(1)}) custom-call(f32[16,16,128]{2,1,0:T(8,128)} %bitcast.19, f32[1,128]{1,0:T(1,128)} %bitcast.29, f32[16,32,128]{2,1,0:T(8,128)} %bitcast.18, f32[16,16,128]{2,1,0:T(8,128)} %bitcast.20, ...), custom_call_target="tpu_custom_call" | custom-call | tf_op jit(solution)/shard_map/pallas_call | solution.py:771
  45.2 0.9 %shard_map.174 = (f32[16,16,128]{2,1,0:T(8,128)}, f32[1,128]{1,0:T(1,128)}, f32[16,32,128]{2,1,0:T(8,128)}, f32[16,16,128]{2,1,0:T(8,128)}, f32[16,16,128]{2,1,0:T(8,128)}) custom-call(f32[16,16,128]{2,1,0:T(8,128)S(1)} %get-tuple-element.15.refs_0_, f32[1,128]{1,0:T(1,128)S(1)} %get-tuple-element.16.refs_1_, f32[16,32,128]{2,1,0:T(8,128)S(1)} %get-tuple-element.17.refs_2_, ...), custom_call_target="tpu_custom_call" | custom-call | tf_op jit(solution)/shard_map/pallas_call | solution.py:819

commit v3 on v2

--- a/solution.py
+++ b/solution.py
@@ -364,7 +364,7 @@
     assert n % 4 == 0 and n & (n - 1) == 0 and sorted(order) == list(range(1, n))
 
     barrier = pltpu.get_barrier_semaphore()
-    for k in order:
+    for k in reversed(range(1, n)):
         pl.semaphore_signal(
             barrier,
             inc=1,
@@ -478,6 +478,7 @@
         grad_src[:, j, :] = dual[:, lanes(j)]
         grad_src[:, bb + j, :] = demand[:, lanes(j)]
     push(lambda peer: grad_src.at[peer], grad_dst, 4)
+    push(lambda peer: lower_hbm.at[peer], lower, 2)
     grad_dst[me] = grad_src[me]
 
     loads["capacity"].wait()
@@ -494,7 +495,6 @@
     cap_src[1:2, :] = 2.0 * trial - old
     push(lambda peer: cap_src, cap_dst, 5)
     cap_dst[me] = cap_src[...]
-    push(lambda peer: lower_hbm.at[peer], lower, 2)
     push(lambda peer: power_hbm.at[peer], power, 3)
 
     for name in ("bus", "leak", "plimit", "start", "limit"):
@@ -577,6 +577,20 @@
         for c in range(0, lines, width):
             advance(ref, c, line_flows(value, c))
 
+    def partial_dual(ref, c):
+        return jnp.dot(
+            ref[:, c : c + width].astype(jnp.bfloat16),
+            shift[c : c + width, :],
+            preferred_element_type=jnp.float32,
+        )
+
+    def flow_step(ref, value):
+        dual = jnp.zeros((n, buses), jnp.float32)
+        for c in range(0, lines, width):
+            advance(ref, c, line_flows(value, c))
+            dual = dual + partial_dual(ref, c)
+        return dual.astype(jnp.bfloat16)
+
     def update_duals(capacity_bar):
         total = jnp.zeros((ub, 128), jnp.float32)
         for t in range(hours):
@@ -637,11 +651,11 @@
     arrive(upper, 1)
     arrive(grad_dst, 4)
     push_flow(0)
+    arrive(lower, 2)
     push_flow(1)
-    arrive(lower, 2)
     push_flow(2)
+    push_flow(3)
     arrive(power, 3)
-    push_flow(3)
     gradient(
         jnp.concatenate([grad_dst[:, j, :] for j in range(bb)], axis=1).astype(jnp.bfloat16)
     )
@@ -653,32 +667,33 @@
     pair_up(0, update_duals(cap_dst[:, 1, :]))
     value = inject(0)
     broadcast(0)
-    send_injection(0)
     adjoints()
     for c in range(0, lines, width):
         flows1[:, c : c + width] = line_flows(value, c)
+    dual = jnp.zeros((n, buses), jnp.float32)
     for q in range(4):
         arrive(flow_in.at[q], (6, 7, 19, 20)[q])
         for j in range(quarter_lb):
             flow[:, lanes(q * quarter_lb + j)] = flow_in[q, :, j, :]
         for c in range(q * quarter_lb * 128, (q + 1) * quarter_lb * 128, width):
             advance(flow, c, flows1[:, c : c + width])
-
-    gradient(bus_dual(flow[...]))
+            dual = dual + partial_dual(flow, c)
+
+    gradient(dual.astype(jnp.bfloat16))
     primal(power, adjoint, first_dst, power)
+    send_injection(0)
     states()
     pair_up(1, update_duals(capacity_step(0)))
     value = inject(1)
     broadcast(1)
     send_injection(1)
     adjoints()
-    lines_step(flow, value)
-
-    gradient(bus_dual(flow[...]))
+    gradient(flow_step(flow, value))
     primal(power, adjoint, first_dst, power)
     push(lambda peer: power.at[peer], power_home, 14)
     power_home[me] = power[me]
     states()
+    lines_step(flow2, injected(0))
     part_src[:, 0, :] = update_duals(capacity_step(1))
     push(lambda peer: part_src.at[peer], part_dst, 13)
     part_dst[me] = part_src[me]
@@ -687,9 +702,7 @@
     send_injection(2)
     push(lambda peer: adjoint.at[peer], adjoint_home, 15)
     adjoint_home[me] = adjoint[me]
-    lines_step(flow, value)
-
-    gradient(bus_dual(flow[...]))
+    gradient(flow_step(flow, value))
     primal(power, adjoint, first_dst, None)
     e = start_in[...]
     for t in range(hours):
@@ -699,6 +712,7 @@
     push(lambda peer: lower.at[peer], lower_out, 16)
     lower_out[me] = lower[me]
     upper_out[me] = upper[me]
+    lines_step(flow2, injected(1))
     arrive(part_dst, 13)
     old = cap_ref[pl.ds(me, 1), :]
     trial = next_capacity(old, my_cost, jnp.sum(part_dst[:, 0, :], axis=0, keepdims=True))
@@ -708,10 +722,7 @@
     push(lambda peer: upper.at[peer], upper_out, 17)
     last_dst[me] = last_src[...]
 
-    lines_step(flow2, injected(0))
-    lines_step(flow2, injected(1))
-    lines_step(flow2, injected(2))
-    gradient(bus_dual(flow2[...]))
+    gradient(flow_step(flow2, injected(2)))
     arrive(power_home, 14)
     arrive(adjoint_home, 15)
     primal(power_home, adjoint_home, first_src, power_out)

time: 46.2 us -> 45.8 us (level)
  no operation moved by 1% of the time
where the time goes in v3:
time: 45.8 us; the launch traced here: 45.7 us
  Pallas kernels  45 us (98%)
  between operations  0.65 us (1%)
    pallas_call x1, Pallas kernels, by_rows(): pl.pallas_call(functools.partial(kernel_rows, n), out_shape=results, in_s...  44.2 us

profile of v3, /device:TPU:0, one launch (start us, length us, event | category | flops | bytes accessed | tf_op | source)
XLA Modules:
  0.0 45.7 jit_solution(9490564412140148537)
XLA Ops:
  0.6 44.2 %shard_map.173 = (f32[16,16,128]{2,1,0:T(8,128)S(1)}, f32[1,128]{1,0:T(1,128)S(1)}, f32[16,32,128]{2,1,0:T(8,128)S(1)}, f32[16,16,128]{2,1,0:T(8,128)S(1)}, f32[16,16,128]{2,1,0:T(8,128)S(1)}) custom-call(f32[16,16,128]{2,1,0:T(8,128)} %bitcast.19, f32[1,128]{1,0:T(1,128)} %bitcast.29, f32[16,32,128]{2,1,0:T(8,128)} %bitcast.18, f32[16,16,128]{2,1,0:T(8,128)} %bitcast.20, ...), custom_call_target="tpu_custom_call" | custom-call | tf_op jit(solution)/shard_map/pallas_call | solution.py:782
  44.8 0.9 %shard_map.174 = (f32[16,16,128]{2,1,0:T(8,128)}, f32[1,128]{1,0:T(1,128)}, f32[16,32,128]{2,1,0:T(8,128)}, f32[16,16,128]{2,1,0:T(8,128)}, f32[16,16,128]{2,1,0:T(8,128)}) custom-call(f32[16,16,128]{2,1,0:T(8,128)S(1)} %get-tuple-element.15.refs_0_, f32[1,128]{1,0:T(1,128)S(1)} %get-tuple-element.16.refs_1_, f32[16,32,128]{2,1,0:T(8,128)S(1)} %get-tuple-element.17.refs_2_, ...), custom_call_target="tpu_custom_call" | custom-call | tf_op jit(solution)/shard_map/pallas_call | solution.py:830

commit v4 on v3

--- a/solution.py
+++ b/solution.py
@@ -340,9 +340,9 @@
         inj_src,
         inj_dst,
         state,
-        power_home,
+        mixed,
         adjoint,
-        adjoint_home,
+        mixed_home,
         cap_ref,
         send_sems,
         recv_sems,
@@ -541,26 +541,23 @@
             e = retain * e - bar[t]
             state[t] = e
 
-    def injection(demand_from):
+    def inject(i):
         for j in range(ub):
             bar16[:, lanes(j)] = bar[:, j, :].astype(jnp.bfloat16)
         value = jnp.dot(bar16[...], inc_t[...], preferred_element_type=jnp.float32)
-        demand = jnp.concatenate([demand_from[:, bb + j, :] for j in range(bb)], axis=1)
-        return (value - demand).astype(jnp.bfloat16)
-
-    def inject(i):
-        value = injection(grad_dst)
+        demand = jnp.concatenate([grad_dst[:, bb + j, :] for j in range(bb)], axis=1)
+        value = (value - demand).astype(jnp.bfloat16)
         wide = value.astype(jnp.float32)
         for j in range(bb):
             inj_src[i, :, j, :] = wide[:, lanes(j)]
         return value
 
     def send_injection(i):
-        push(lambda peer: inj_src.at[i, peer], inj_dst.at[i], 8 + i)
+        push(lambda peer: inj_src.at[i, peer], inj_dst.at[i], (8, 9, 10, 14)[i])
         inj_dst[i, me] = inj_src[i, me]
 
     def injected(i):
-        arrive(inj_dst.at[i], 8 + i)
+        arrive(inj_dst.at[i], (8, 9, 10, 14)[i])
         return jnp.concatenate([inj_dst[i, :, j, :] for j in range(bb)], axis=1).astype(
             jnp.bfloat16
         )
@@ -690,18 +687,17 @@
     adjoints()
     gradient(flow_step(flow, value))
     primal(power, adjoint, first_dst, power)
-    push(lambda peer: power.at[peer], power_home, 14)
-    power_home[me] = power[me]
     states()
-    lines_step(flow2, injected(0))
     part_src[:, 0, :] = update_duals(capacity_step(1))
     push(lambda peer: part_src.at[peer], part_dst, 13)
     part_dst[me] = part_src[me]
     adjoints()
+    for t in range(hours):
+        mixed[t] = power[t] + primal_step * adjoint[t]
+    push(lambda peer: mixed.at[peer], mixed_home, 15)
+    mixed_home[me] = mixed[me]
     value = inject(2)
     send_injection(2)
-    push(lambda peer: adjoint.at[peer], adjoint_home, 15)
-    adjoint_home[me] = adjoint[me]
     gradient(flow_step(flow, value))
     primal(power, adjoint, first_dst, None)
     e = start_in[...]
@@ -709,10 +705,12 @@
         e = retain * e - bar[t]
         lower[t] = jnp.maximum(lower[t] - dual_step * e, 0.0)
         upper[t] = upper[t] + dual_step * e
+    inject(3)
+    send_injection(3)
     push(lambda peer: lower.at[peer], lower_out, 16)
     lower_out[me] = lower[me]
     upper_out[me] = upper[me]
-    lines_step(flow2, injected(1))
+    lines_step(flow2, injected(0))
     arrive(part_dst, 13)
     old = cap_ref[pl.ds(me, 1), :]
     trial = next_capacity(old, my_cost, jnp.sum(part_dst[:, 0, :], axis=0, keepdims=True))
@@ -722,11 +720,14 @@
     push(lambda peer: upper.at[peer], upper_out, 17)
     last_dst[me] = last_src[...]
 
+    lines_step(flow2, injected(1))
     gradient(flow_step(flow2, injected(2)))
-    arrive(power_home, 14)
-    arrive(adjoint_home, 15)
-    primal(power_home, adjoint_home, first_src, power_out)
-    lines_step(flow2, injection(grad_src))
+    arrive(mixed_home, 15)
+    for s in range(scen):
+        power_out[s] = jnp.clip(
+            mixed_home[s] - primal_step * (grid[s] - first_src[s, 1:2, :]), -plimit, plimit
+        )
+    lines_step(flow2, injected(3))
     for j in range(lb):
         flow_out[:, j, :] = flow2[:, lanes(j)]
     arrive(lower_out, 16)
@@ -739,7 +740,7 @@
         [first_dst, upper, lower, power, grad_dst, cap_dst, flow_in.at[0], flow_in.at[1]]
         + [inj_dst.at[i] for i in range(3)]
         + [total_dst.at[i] for i in range(2)]
-        + [part_dst, power_home, adjoint_home, lower_out, upper_out, last_dst]
+        + [part_dst, inj_dst.at[3], mixed_home, lower_out, upper_out, last_dst]
         + [flow_in.at[2], flow_in.at[3]]
     )
     for channel, dst in enumerate(sent):
@@ -809,8 +810,8 @@
             buffer(n, 1, 128),
             buffer(1, 128),
             buffer(n, 1, 128),
-            buffer(3, n, bb, 128),
-            buffer(3, n, bb, 128),
+            buffer(4, n, bb, 128),
+            buffer(4, n, bb, 128),
             buffer(*state),
             buffer(*state),
             buffer(*state),

time: 45.8 us -> 45.3 us (0.989)
  Pallas kernels: 45 us -> 44.5 us
    pallas_call x1, Pallas kernels: 44.2 us -> 43.6 us  [by_rows(): pl.pallas_call(functools.partial(kernel_rows, n), out_shape=results, in_s...]
where the time goes in v4:
time: 45.3 us; the launch traced here: 45.1 us
  Pallas kernels  44.5 us (98%)
  between operations  0.65 us (1%)
    pallas_call x1, Pallas kernels, by_rows(): pl.pallas_call(functools.partial(kernel_rows, n), out_shape=results, in_s...  43.6 us

profile of v4, /device:TPU:0, one launch (start us, length us, event | category | flops | bytes accessed | tf_op | source)
XLA Modules:
  0.0 45.1 jit_solution(8645645412355832534)
XLA Ops:
  0.6 43.6 %shard_map.173 = (f32[16,16,128]{2,1,0:T(8,128)S(1)}, f32[1,128]{1,0:T(1,128)S(1)}, f32[16,32,128]{2,1,0:T(8,128)S(1)}, f32[16,16,128]{2,1,0:T(8,128)S(1)}, f32[16,16,128]{2,1,0:T(8,128)S(1)}) custom-call(f32[16,16,128]{2,1,0:T(8,128)} %bitcast.19, f32[1,128]{1,0:T(1,128)} %bitcast.29, f32[16,32,128]{2,1,0:T(8,128)} %bitcast.18, f32[16,16,128]{2,1,0:T(8,128)} %bitcast.20, ...), custom_call_target="tpu_custom_call" | custom-call | tf_op jit(solution)/shard_map/pallas_call | solution.py:783
  44.2 0.9 %shard_map.174 = (f32[16,16,128]{2,1,0:T(8,128)}, f32[1,128]{1,0:T(1,128)}, f32[16,32,128]{2,1,0:T(8,128)}, f32[16,16,128]{2,1,0:T(8,128)}, f32[16,16,128]{2,1,0:T(8,128)}) custom-call(f32[16,16,128]{2,1,0:T(8,128)S(1)} %get-tuple-element.15.refs_0_, f32[1,128]{1,0:T(1,128)S(1)} %get-tuple-element.16.refs_1_, f32[16,32,128]{2,1,0:T(8,128)S(1)} %get-tuple-element.17.refs_2_, ...), custom_call_target="tpu_custom_call" | custom-call | tf_op jit(solution)/shard_map/pallas_call | solution.py:831

commit v5 on v4

--- a/solution.py
+++ b/solution.py
@@ -688,6 +688,8 @@
     gradient(flow_step(flow, value))
     primal(power, adjoint, first_dst, power)
     states()
+    value = inject(2)
+    send_injection(2)
     part_src[:, 0, :] = update_duals(capacity_step(1))
     push(lambda peer: part_src.at[peer], part_dst, 13)
     part_dst[me] = part_src[me]
@@ -696,8 +698,6 @@
         mixed[t] = power[t] + primal_step * adjoint[t]
     push(lambda peer: mixed.at[peer], mixed_home, 15)
     mixed_home[me] = mixed[me]
-    value = inject(2)
-    send_injection(2)
     gradient(flow_step(flow, value))
     primal(power, adjoint, first_dst, None)
     e = start_in[...]

time: 45.3 us -> 44.6 us (0.985)
  Pallas kernels: 44.5 us -> 43.8 us
    pallas_call x1, Pallas kernels: 43.6 us -> 42.9 us  [by_rows(): pl.pallas_call(functools.partial(kernel_rows, n), out_shape=results, in_s...]
where the time goes in v5:
time: 44.6 us; the launch traced here: 44.4 us
  Pallas kernels  43.8 us (98%)
  between operations  0.65 us (1%)
    pallas_call x1, Pallas kernels, by_rows(): pl.pallas_call(functools.partial(kernel_rows, n), out_shape=results, in_s...  42.9 us

profile of v5, /device:TPU:0, one launch (start us, length us, event | category | flops | bytes accessed | tf_op | source)
XLA Modules:
  0.0 44.4 jit_solution(8018191425769274802)
XLA Ops:
  0.6 42.9 %shard_map.173 = (f32[16,16,128]{2,1,0:T(8,128)S(1)}, f32[1,128]{1,0:T(1,128)S(1)}, f32[16,32,128]{2,1,0:T(8,128)S(1)}, f32[16,16,128]{2,1,0:T(8,128)S(1)}, f32[16,16,128]{2,1,0:T(8,128)S(1)}) custom-call(f32[16,16,128]{2,1,0:T(8,128)} %bitcast.19, f32[1,128]{1,0:T(1,128)} %bitcast.29, f32[16,32,128]{2,1,0:T(8,128)} %bitcast.18, f32[16,16,128]{2,1,0:T(8,128)} %bitcast.20, ...), custom_call_target="tpu_custom_call" | custom-call | tf_op jit(solution)/shard_map/pallas_call | solution.py:783
  43.5 0.9 %shard_map.174 = (f32[16,16,128]{2,1,0:T(8,128)}, f32[1,128]{1,0:T(1,128)}, f32[16,32,128]{2,1,0:T(8,128)}, f32[16,16,128]{2,1,0:T(8,128)}, f32[16,16,128]{2,1,0:T(8,128)}) custom-call(f32[16,16,128]{2,1,0:T(8,128)S(1)} %get-tuple-element.15.refs_0_, f32[1,128]{1,0:T(1,128)S(1)} %get-tuple-element.16.refs_1_, f32[16,32,128]{2,1,0:T(8,128)S(1)} %get-tuple-element.17.refs_2_, ...), custom_call_target="tpu_custom_call" | custom-call | tf_op jit(solution)/shard_map/pallas_call | solution.py:831
